TPU v7x, 32 devices: a whole 2x2x4 slice. The times are simulated.
32 devices in a mesh: row: 8 (over z, y), col: 4 (over x, core).
Axes of the slice: x: 2, y: 2, z: 4, core: 2. Of those that a mesh axis runs over, the one named last changes fastest.
Arguments:
- activations: bfloat16 [512, 28672], P('col', 'row'), may hold values from -36 to 36
- output_gradient: bfloat16 [512, 8192], P('row', 'col'), may hold values from -6 to 6
- frozen_weight: bfloat16 [28672, 8192], P('row', 'col'), may hold values from -0.0390625 to 0.0390625
- sparsity_mask_pattern: int32 [7168, 8192], P('row', 'col'), may hold values from 0 to 5
- adapter_left_factor: bfloat16 [28672, 16], P('row'), may hold values from -0.19921875 to 0.19921875
- adapter_right_factor: bfloat16 [16, 8192], P(None, 'col'), may hold values from -0.359375 to 0.359375
Outputs:
- input_grad: bfloat16 [512, 28672], P('col', 'row')
- left_grad: float32 [28672, 16], P('row')
- right_grad: float32 [16, 8192], P(None, 'col')
Inputs may be any that keep to these rules, and one draw needn't show every extreme that they name: `sparsity_mask_pattern`: a pattern number of the 2:4 mask.
All inputs are finite; a program needn't handle non-finite values.
Results may differ from a plain program's by a relative error of at most 0.005.
Values may be sent and summed in bfloat16 or wider, within the bound.
No kernel may reach another device: no remote copies, remote signals or barrier semaphores. Data moves between devices by JAX's collectives and lax.ppermute only.
A program may use at most 192 MiB of HBM per device.

v0:
```python
import jax
import jax.numpy as jnp
from jax import lax
from jax.sharding import PartitionSpec as P

PAIRS = ((0, 1), (0, 2), (0, 3), (1, 2), (1, 3), (2, 3))
ADAPTER_SCALE = 2.0


def expand_mask(code):
    groups = []
    for column in range(4):
        kept = jnp.zeros(code.shape, jnp.float32)
        for pattern in range(6):
            if column in PAIRS[pattern]:
                kept = kept + (code == pattern).astype(jnp.float32)
        groups.append(kept)
    stacked = jnp.stack(groups, axis=1)
    return stacked.reshape(code.shape[0] * 4, code.shape[1])


def input_sums_of(grad_rows, merged):
    return lax.psum_scatter(
        lax.dot_general(
            grad_rows, merged, (((1,), (1,)), ((), ())), preferred_element_type=jnp.float32
        ),
        "col",
        scatter_dimension=0,
        tiled=True,
    )


def weight_grad_of(activations, grad_rows):
    return lax.dot_general(
        lax.all_gather(activations, "col", axis=0, tiled=True),
        grad_rows,
        (((0,), (0,)), ((), ())),
        preferred_element_type=jnp.float32,
    )


def per_device(
    activations,
    output_gradient,
    frozen_weight,
    sparsity_mask_pattern,
    adapter_left_factor,
    adapter_right_factor,
):
    masked = expand_mask(sparsity_mask_pattern)
    low_rank_update = jnp.dot(
        adapter_left_factor, adapter_right_factor, preferred_element_type=jnp.float32
    )
    merged = (
        masked * (frozen_weight.astype(jnp.float32) + ADAPTER_SCALE * low_rank_update)
    ).astype(jnp.bfloat16)
    grad_rows = lax.all_gather(output_gradient, "row", axis=0, tiled=True)
    all_tokens = grad_rows.shape[0]
    first_grad = weight_grad_of(activations, grad_rows)
    weight_grad, later_grads = lax.optimization_barrier((first_grad, grad_rows))
    input_grad = input_sums_of(later_grads, merged).astype(jnp.bfloat16)
    pruned_gradient = (masked * weight_grad / all_tokens).astype(jnp.bfloat16)
    left_partial = ADAPTER_SCALE * lax.dot_general(
        pruned_gradient,
        adapter_right_factor,
        (((1,), (1,)), ((), ())),
        preferred_element_type=jnp.float32,
    )
    right_partial = ADAPTER_SCALE * lax.dot_general(
        adapter_left_factor,
        pruned_gradient,
        (((0,), (0,)), ((), ())),
        preferred_element_type=jnp.float32,
    )
    right_grad = lax.psum(right_partial, "row")
    left_grad = lax.psum(left_partial, "col")
    return (input_grad, left_grad, right_grad)


def solution(mesh):
    in_specs = (
        P("col", "row"),
        P("row", "col"),
        P("row", "col"),
        P("row", "col"),
        P("row", None),
        P(None, "col"),
    )
    out_specs = (P("col", "row"), P("row", None), P(None, "col"))
    return jax.shard_map(
        per_device, mesh=mesh, in_specs=in_specs, out_specs=out_specs, check_vma=False
    )
```

profile of v0, /device:TPU:0, one launch (start us, length us, event | category | flops | bytes accessed | tf_op | source)
XLA Modules:
  0.0 334.8 jit_solution(17214782488458227821)
XLA Ops:
  7.2 0.0 copy-start
  7.2 0.0 all-gather.5.cloned.1.call-start
  7.2 0.7 all-gather.5.cloned.1.call-update
  7.9 0.0 all-gather.3.cloned.1.call-start
  8.0 0.7 all-gather.3.cloned.1.call-update
  8.7 0.0 reduce-scatter.2.cloned.1.call-start
  8.7 0.0 slice-start
  8.7 7.8 %fusion = (f32[896,1,2048]{2,0,1:T(8,128)S(1)}, pred[896,2048]{1,0:T(8,128)(4,1)S(1)}, pred[896,2048]{1,0:T(8,128)(4,1)S(1)}, pred[896,2048]{1,0:T(8,128)(4,1)}) fusion(s32[896,2048]{1,0:T(8,128)} %param.9), kind=kLoop, calls=%fused_computation.11 | loop fusion | flops 14680064 | bytes 20185088 | tf_op jit(solution)/shard_map/stack | solution.py:18
  16.5 0.0 slice-start.1
  16.6 6.5 %fusion.1 = (f32[896,1,2048]{2,0,1:T(8,128)S(1)}, pred[896,2048]{1,0:T(8,128)(4,1)S(1)}, pred[896,2048]{1,0:T(8,128)(4,1)}) fusion(pred[896,2048]{1,0:T(8,128)(4,1)S(1)} %get-tuple-element.8, s32[896,2048]{1,0:T(8,128)} %param.9), kind=kLoop, calls=%fused_computation.12 | loop fusion | flops 12845056 | bytes 20185088 | tf_op jit(solution)/shard_map/stack | solution.py:18
  23.1 0.0 slice-done
  23.1 0.0 slice-done.1
  23.1 3.6 %fusion.2 = (f32[896,1,2048]{2,0,1:T(8,128)S(1)}, pred[896,2048]{1,0:T(8,128)(4,1)}) fusion(pred[896,2048]{1,0:T(8,128)(4,1)S(1)} %get-tuple-element.12, pred[896,2048]{1,0:T(8,128)(4,1)S(1)} %get-tuple-element.9, s32[896,2048]{1,0:T(8,128)S(1)} %bitcast.20), kind=kLoop, calls=%fused_computation.13 | loop fusion | flops 11010048 | bytes 20185088 | tf_op jit(solution)/shard_map/stack | solution.py:18
  26.7 5.1 %fusion.3 = f32[896,1,2048]{2,0,1:T(8,128)S(1)} fusion(pred[896,2048]{1,0:T(8,128)(4,1)} %get-tuple-element.15, pred[896,2048]{1,0:T(8,128)(4,1)} %get-tuple-element.13, pred[896,2048]{1,0:T(8,128)(4,1)} %get-tuple-element.10), kind=kLoop, calls=%fused_computation.14 | loop fusion | flops 9175040 | bytes 12845056 | tf_op jit(solution)/shard_map/stack | solution.py:18
  31.8 10.3 %pad_maximum_fusion = f32[896,4,2048]{2,0,1:T(8,128)} fusion(f32[896,1,2048]{2,0,1:T(8,128)S(1)} %fusion.3, f32[896,1,2048]{2,0,1:T(8,128)S(1)} %get-tuple-element.14, f32[896,1,2048]{2,0,1:T(8,128)S(1)} %get-tuple-element.11, f32[896,1,2048]{2,0,1:T(8,128)S(1)} %get-tuple-element.7), kind=kLoop, calls=%fused_computation | loop fusion | flops 22020096 | bytes 58720256 | tf_op jit(solution)/shard_map/stack | solution.py:18
  42.1 33.6 %copy.9 = f32[896,4,2048]{2,1,0:T(4,128)} copy(f32[896,4,2048]{2,0,1:T(8,128)} %pad_maximum_fusion) | data formatting | bytes 58720256 | tf_op jit(solution)/shard_map/stack | solution.py:18
  75.7 33.5 %reshape.9 = f32[3584,2048]{1,0:T(8,128)} reshape(f32[896,4,2048]{2,1,0:T(4,128)} %copy.9) | data formatting | bytes 58720256 | tf_op jit(solution)/shard_map/reshape | solution.py:19
  109.2 0.0 copy-start.1
  109.2 0.0 all-gather.5.cloned.1.call-done
  109.2 0.0 copy-start.2
  109.2 0.0 all-gather.3.cloned.1.call-done
  109.2 16.2 %fusion.7 = f32[3584,2048]{1,0:T(8,128)} fusion(bf16[512,3584]{1,0:T(8,128)(2,1)} %all-gather.3.cloned.1.call-done, bf16[512,2048]{1,0:T(8,128)(2,1)} %all-gather.5.cloned.1.call-done), kind=kOutput, calls=%fused_computation.26 | convolution fusion | flops 7516192768 | bytes 35127296 | tf_op jit(solution)/shard_map/dot_general | solution.py:34
  125.4 0.0 copy-done
  125.4 0.0 copy-done.1
  125.4 0.0 copy-done.2
  125.4 21.5 %fusion.4 = f32[512,3584]{1,0:T(8,128)} fusion(bf16[512,2048]{1,0:T(8,128)(2,1)S(1)} %copy-done.2, f32[3584,2048]{1,0:T(8,128)} %reshape.9, bf16[3584,2048]{1,0:T(8,128)(2,1)} %param.8, bf16[3584,16]{0,1:T(8,128)(2,1)S(1)} %copy-done, bf16[16,2048]{1,0:T(8,128)(2,1)S(1)} %copy-done.1), kind=kOutput, calls=%fused_computation.22 | convolution fusion | flops 7787773952 | bytes 53657600 | tf_op jit(solution)/shard_map/dot_general | solution.py:24
  146.9 0.0 reduce-scatter.2.cloned.1.call-update
  147.0 0.0 all-reduce.3.cloned.1.call-start
  147.0 26.9 %multiply_convert_fusion = bf16[3584,2048]{1,0:T(8,128)(2,1)} fusion(f32[3584,2048]{1,0:T(8,128)} %reshape.9, f32[3584,2048]{1,0:T(8,128)} %fusion.7), kind=kLoop, calls=%fused_computation.1 | loop fusion | flops 22020096 | bytes 73400320 | tf_op jit(solution)/shard_map/convert_element_type | solution.py:62
  173.9 9.9 %convolution_multiply_fusion = f32[3584,16]{0,1:T(8,128)} fusion(bf16[3584,2048]{1,0:T(8,128)(2,1)} %multiply_convert_fusion, bf16[16,2048]{1,0:T(8,128)(2,1)S(1)} %copy-done.1), kind=kOutput, calls=%fused_computation.15 | convolution fusion | flops 234938368 | bytes 14974976 | tf_op jit(solution)/shard_map/dot_general | solution.py:63
  183.8 0.0 all-reduce.3.cloned.1.call-update
  183.8 0.0 all-reduce.5.cloned.1.call-start
  183.9 8.0 %fusion.5 = f32[16,2048]{1,0:T(8,128)} fusion(bf16[3584,16]{0,1:T(8,128)(2,1)S(1)} %copy-done, bf16[3584,2048]{1,0:T(8,128)(2,1)} %multiply_convert_fusion), kind=kOutput, calls=%fused_computation.24 | convolution fusion | flops 234913792 | bytes 14925824 | tf_op jit(solution)/shard_map/dot_general | solution.py:69
  191.9 0.0 all-reduce.5.cloned.1.call-update
  191.9 24.0 %reduce-scatter.2.cloned.1.call-done = f32[128,3584]{1,0:T(8,128)} async-done(((f32[512,3584]{1,0:T(8,128)}), f32[128,3584]{1,0:T(8,128)}) %reduce-scatter.2.cloned.1.call-update) | async-done | bytes 1835024 | tf_op jit(solution)/shard_map/reduce_scatter | solution.py:23
  215.9 2.5 convert_element_type.44
  218.4 32.5 %all-reduce.3.cloned.1.call-done = f32[3584,16]{0,1:T(8,128)} async-done(((f32[3584,16]{0,1:T(8,128)}), f32[3584,16]{0,1:T(8,128)}) %all-reduce.3.cloned.1.call-update) | async-done | bytes 229392 | tf_op jit(solution)/shard_map/psum | solution.py:76
  250.9 74.2 %all-reduce.5.cloned.1.call-done = f32[16,2048]{1,0:T(8,128)} async-done(((f32[16,2048]{1,0:T(8,128)}), f32[16,2048]{1,0:T(8,128)}) %all-reduce.5.cloned.1.call-update) | async-done | bytes 131088 | tf_op jit(solution)/shard_map/psum | solution.py:75
  325.0 1.6 copy.12
  326.7 1.6 copy.13
  (1 shorter events, 0.0 us)
Async XLA Ops:
  7.2 118.2 %copy-start = (bf16[3584,16]{0,1:T(8,128)(2,1)S(1)}, bf16[3584,16]{0,1:T(8,128)(2,1)}, u32[]{:S(2)}) copy-start(bf16[3584,16]{0,1:T(8,128)(2,1)} %param.10) | copy-start | bytes 344068
  7.2 102.0 %all-gather.5.cloned.1.call-start = ((), (), s32[]{:S(2)}) async-start(), calls=%async_computation.2 | async-start | bytes 2359296 | tf_op jit(solution)/shard_map/all_gather | solution.py:57
  7.9 101.3 %all-gather.3.cloned.1.call-start = ((), (), s32[]{:S(2)}) async-start(), calls=%async_computation.1 | async-start | bytes 4587520 | tf_op jit(solution)/shard_map/all_gather | solution.py:35
  8.7 207.2 %reduce-scatter.2.cloned.1.call-start = ((), (), s32[]{:S(2)}) async-start(), calls=%async_computation.3 | async-start | bytes 9175040 | tf_op jit(solution)/shard_map/reduce_scatter | solution.py:23
  8.7 14.4 %slice-start = ((s8[7340032]{0:T(1024)(128)(4,1)}), s8[4194304]{0:T(1024)(128)(4,1)S(1)}, s32[]{:S(2)}) async-start(s8[7340032]{0:T(1024)(128)(4,1)} %bitcast.19), calls=%async_computation.6 | async-start | bytes 8388608
  16.5 6.5 %slice-start.1 = ((s8[7340032]{0:T(1024)(128)(4,1)}), s8[3145728]{0:T(1024)(128)(4,1)S(1)}, s32[]{:S(2)}) async-start(s8[7340032]{0:T(1024)(128)(4,1)} %bitcast.19), calls=%async_computation.7 | async-start | bytes 6291456
  109.2 16.2 %copy-start.1 = (bf16[16,2048]{1,0:T(8,128)(2,1)S(1)}, bf16[16,2048]{1,0:T(8,128)(2,1)}, u32[]{:S(2)}) copy-start(bf16[16,2048]{1,0:T(8,128)(2,1)} %param.11) | copy-start | bytes 196612
  109.2 16.2 %copy-start.2 = (bf16[512,2048]{1,0:T(8,128)(2,1)S(1)}, bf16[512,2048]{1,0:T(8,128)(2,1)}, u32[]{:S(2)}) copy-start(bf16[512,2048]{1,0:T(8,128)(2,1)} %all-gather.5.cloned.1.call-done) | copy-start | bytes 6291460
  147.0 103.9 %all-reduce.3.cloned.1.call-start = ((), (), s32[]{:S(2)}) async-start(), calls=%async_computation.4 | async-start | bytes 458752 | tf_op jit(solution)/shard_map/psum | solution.py:76
  183.8 141.2 %all-reduce.5.cloned.1.call-start = ((), (), s32[]{:S(2)}) async-start(), calls=%async_computation.5 | async-start | bytes 262144 | tf_op jit(solution)/shard_map/psum | solution.py:75
Sparse Core Ops, SparseCore 0:
  10.1 51.8 all-gather.4
  63.5 29.9 all-gather.2
  147.1 68.7 reduce-scatter.1
  218.6 32.1 all-reduce.2
  254.6 70.3 all-reduce.4
where the time goes:
time: 336 us; the launch traced here: 335 us
  waiting for transfers between devices  132 us (39%)
  local copies, waits for them, and re-layouts  70.4 us (21%)
  other arithmetic  62.8 us (19%)
  matrix products  55.6 us (17%)
  between operations  13.8 us (4%)
    psum x1, waiting for transfers between devices, per_device(): right_grad = lax.psum(right_partial, 'row')  74.2 us
    another operation x1, local copies, waits for them, and re-layouts, expand_mask(): stacked = jnp.stack(groups, axis=1)  33.6 us
    reshape x1, local copies, waits for them, and re-layouts, expand_mask(): return stacked.reshape(code.shape[0] * 4, code.shape[1])  33.5 us
    another operation x5, other arithmetic, expand_mask(): stacked = jnp.stack(groups, axis=1)  33.3 us
    psum x1, waiting for transfers between devices, per_device(): left_grad = lax.psum(left_partial, 'col')  32.5 us
    convert_element_type x1, other arithmetic, per_device(): pruned_gradient = (masked * weight_grad / all_tokens).astype(jnp.bfloat16)  26.9 us
    reduce_scatter x1, waiting for transfers between devices, input_sums_of(): lax.psum_scatter(lax.dot_general(grad_rows, merged, (((1,), (1,)), ((), (...  24 us
    dot_general x1, matrix products, input_sums_of(): lax.dot_general(grad_rows, merged, (((1,), (1,)), ((), ())), preferred_el...  21.5 us
  transfers between devices with their start and end apart: 5, of which 3 were waited for; matrix products, arithmetic and copies ran while one was open for 44% of the time, Pallas kernels for 0%

commit v1 on v0

--- a/solution.py
+++ b/solution.py
@@ -72,7 +72,8 @@
         (((0,), (0,)), ((), ())),
         preferred_element_type=jnp.float32,
     )
-    right_grad = lax.psum(right_partial, "row")
+    blocks = lax.all_gather(right_partial, "row")
+    right_grad = jnp.sum(blocks, axis=0)
     left_grad = lax.psum(left_partial, "col")
     return (input_grad, left_grad, right_grad)
 

time: 336 us -> 313 us (0.932)
  waiting for transfers between devices: 132 us -> 111 us
    psum x1 -> x0, waiting for transfers between devices: 74.2 us -> none  [per_device(): right_grad = lax.psum(right_partial, 'row')]
    reduce_scatter x1, waiting for transfers between devices: 24 us -> 65.2 us  [input_sums_of(): lax.psum_scatter(lax.dot_general(grad_rows, merged, (((1,), (1,)), ((), (...]
    all_gather x0 -> x1, waiting for transfers between devices: none -> 11.5 us  [per_device(): blocks = lax.all_gather(right_partial, 'row')]
where the time goes in v1:
time: 313 us; the launch traced here: 312 us
  waiting for transfers between devices  111 us (35%)
  local copies, waits for them, and re-layouts  68.8 us (22%)
  other arithmetic  63 us (20%)
  matrix products  55.1 us (18%)
  between operations  13.8 us (4%)
    reduce_scatter x1, waiting for transfers between devices, input_sums_of(): lax.psum_scatter(lax.dot_general(grad_rows, merged, (((1,), (1,)), ((), (...  65.2 us
    another operation x5, other arithmetic, expand_mask(): stacked = jnp.stack(groups, axis=1)  33.8 us
    another operation x1, local copies, waits for them, and re-layouts, expand_mask(): stacked = jnp.stack(groups, axis=1)  33.6 us
    reshape x1, local copies, waits for them, and re-layouts, expand_mask(): return stacked.reshape(code.shape[0] * 4, code.shape[1])  33.5 us
    psum x1, waiting for transfers between devices, per_device(): left_grad = lax.psum(left_partial, 'col')  32.5 us
    convert_element_type x1, other arithmetic, per_device(): pruned_gradient = (masked * weight_grad / all_tokens).astype(jnp.bfloat16)  24.7 us
    dot_general x1, matrix products, input_sums_of(): lax.dot_general(grad_rows, merged, (((1,), (1,)), ((), ())), preferred_el...  21.5 us
    dot_general x1, matrix products, weight_grad_of(): lax.dot_general(lax.all_gather(activations, 'col', axis=0, tiled=True), g...  15.8 us
  transfers between devices with their start and end apart: 5, of which 3 were waited for; matrix products, arithmetic and copies ran while one was open for 44% of the time, Pallas kernels for 0%

profile of v1, /device:TPU:0, one launch (start us, length us, event | category | flops | bytes accessed | tf_op | source)
XLA Modules:
  0.0 311.7 jit_solution(6069649873027656312)
XLA Ops:
  7.2 0.0 copy-start
  7.2 0.0 all-gather.7.cloned.1.call-start
  7.2 0.7 all-gather.7.cloned.1.call-update
  7.9 0.0 all-gather.5.cloned.1.call-start
  8.0 0.7 all-gather.5.cloned.1.call-update
  8.7 0.0 all-gather.9.cloned.1.call-start
  8.7 0.0 slice-start
  8.7 7.6 %fusion = (f32[896,1,2048]{2,0,1:T(8,128)S(1)}, pred[896,2048]{1,0:T(8,128)(4,1)S(1)}, pred[896,2048]{1,0:T(8,128)(4,1)S(1)}, pred[896,2048]{1,0:T(8,128)(4,1)}) fusion(s32[896,2048]{1,0:T(8,128)} %param.9), kind=kLoop, calls=%fused_computation.11 | loop fusion | flops 14680064 | bytes 20185088 | tf_op jit(solution)/shard_map/stack | solution.py:18
  16.4 0.0 slice-start.1
  16.4 6.5 %fusion.1 = (f32[896,1,2048]{2,0,1:T(8,128)S(1)}, pred[896,2048]{1,0:T(8,128)(4,1)S(1)}, pred[896,2048]{1,0:T(8,128)(4,1)}) fusion(pred[896,2048]{1,0:T(8,128)(4,1)S(1)} %get-tuple-element.8, s32[896,2048]{1,0:T(8,128)} %param.9), kind=kLoop, calls=%fused_computation.12 | loop fusion | flops 12845056 | bytes 20185088 | tf_op jit(solution)/shard_map/stack | solution.py:18
  22.9 0.0 slice-done
  22.9 0.0 slice-done.1
  22.9 3.6 %fusion.2 = (f32[896,1,2048]{2,0,1:T(8,128)S(1)}, pred[896,2048]{1,0:T(8,128)(4,1)}) fusion(pred[896,2048]{1,0:T(8,128)(4,1)S(1)} %get-tuple-element.12, pred[896,2048]{1,0:T(8,128)(4,1)S(1)} %get-tuple-element.9, s32[896,2048]{1,0:T(8,128)S(1)} %bitcast.21), kind=kLoop, calls=%fused_computation.13 | loop fusion | flops 11010048 | bytes 20185088 | tf_op jit(solution)/shard_map/stack | solution.py:18
  26.5 5.1 %fusion.3 = f32[896,1,2048]{2,0,1:T(8,128)S(1)} fusion(pred[896,2048]{1,0:T(8,128)(4,1)} %get-tuple-element.15, pred[896,2048]{1,0:T(8,128)(4,1)} %get-tuple-element.13, pred[896,2048]{1,0:T(8,128)(4,1)} %get-tuple-element.10), kind=kLoop, calls=%fused_computation.14 | loop fusion | flops 9175040 | bytes 12845056 | tf_op jit(solution)/shard_map/stack | solution.py:18
  31.6 11.0 %pad_maximum_fusion = f32[896,4,2048]{2,0,1:T(8,128)} fusion(f32[896,1,2048]{2,0,1:T(8,128)S(1)} %fusion.3, f32[896,1,2048]{2,0,1:T(8,128)S(1)} %get-tuple-element.14, f32[896,1,2048]{2,0,1:T(8,128)S(1)} %get-tuple-element.11, f32[896,1,2048]{2,0,1:T(8,128)S(1)} %get-tuple-element.7), kind=kLoop, calls=%fused_computation | loop fusion | flops 22020096 | bytes 58720256 | tf_op jit(solution)/shard_map/stack | solution.py:18
  42.5 33.6 %copy.9 = f32[896,4,2048]{2,1,0:T(4,128)} copy(f32[896,4,2048]{2,0,1:T(8,128)} %pad_maximum_fusion) | data formatting | bytes 58720256 | tf_op jit(solution)/shard_map/stack | solution.py:18
  76.1 33.5 %reshape.9 = f32[3584,2048]{1,0:T(8,128)} reshape(f32[896,4,2048]{2,1,0:T(4,128)} %copy.9) | data formatting | bytes 58720256 | tf_op jit(solution)/shard_map/reshape | solution.py:19
  109.7 0.0 all-gather.7.cloned.1.call-done
  109.7 0.0 all-gather.5.cloned.1.call-done
  109.7 15.8 %fusion.7 = f32[3584,2048]{1,0:T(8,128)} fusion(bf16[512,3584]{1,0:T(8,128)(2,1)} %all-gather.5.cloned.1.call-done, bf16[512,2048]{1,0:T(8,128)(2,1)} %all-gather.7.cloned.1.call-done), kind=kOutput, calls=%fused_computation.26 | convolution fusion | flops 7516192768 | bytes 35127296 | tf_op jit(solution)/shard_map/dot_general | solution.py:34
  125.5 24.7 %multiply_convert_fusion = bf16[3584,2048]{1,0:T(8,128)(2,1)} fusion(f32[3584,2048]{1,0:T(8,128)} %reshape.9, f32[3584,2048]{1,0:T(8,128)} %fusion.7), kind=kLoop, calls=%fused_computation.1 | loop fusion | flops 22020096 | bytes 73400320 | tf_op jit(solution)/shard_map/convert_element_type | solution.py:62
  150.2 0.0 copy-done
  150.2 0.0 copy-start.1
  150.2 0.0 copy-start.2
  150.2 8.0 %fusion.5 = f32[16,2048]{1,0:T(8,128)} fusion(bf16[3584,16]{0,1:T(8,128)(2,1)S(1)} %copy-done, bf16[3584,2048]{1,0:T(8,128)(2,1)} %multiply_convert_fusion), kind=kOutput, calls=%fused_computation.24 | convolution fusion | flops 234913792 | bytes 14925824 | tf_op jit(solution)/shard_map/dot_general | solution.py:69
  158.2 0.0 all-gather.9.cloned.1.call-update
  158.2 0.0 reduce-scatter.2.cloned.1.call-start
  158.3 0.0 copy-done.1
  158.3 0.0 copy-done.2
  158.3 21.5 %fusion.4 = f32[512,3584]{1,0:T(8,128)} fusion(bf16[512,2048]{1,0:T(8,128)(2,1)S(1)} %copy-done.2, f32[3584,2048]{1,0:T(8,128)} %reshape.9, bf16[3584,2048]{1,0:T(8,128)(2,1)} %param.8, bf16[3584,16]{0,1:T(8,128)(2,1)S(1)} %copy-done, bf16[16,2048]{1,0:T(8,128)(2,1)S(1)} %copy-done.1), kind=kOutput, calls=%fused_computation.22 | convolution fusion | flops 7787773952 | bytes 53657600 | tf_op jit(solution)/shard_map/dot_general | solution.py:24
  179.8 0.0 reduce-scatter.2.cloned.1.call-update
  179.8 0.3 all-reduce.2.cloned.1.call-start
  180.1 9.8 %convolution_multiply_fusion = f32[3584,16]{0,1:T(8,128)} fusion(bf16[3584,2048]{1,0:T(8,128)(2,1)} %multiply_convert_fusion, bf16[16,2048]{1,0:T(8,128)(2,1)S(1)} %copy-done.1), kind=kOutput, calls=%fused_computation.15 | convolution fusion | flops 234938368 | bytes 14974976 | tf_op jit(solution)/shard_map/dot_general | solution.py:63
  189.8 0.0 all-reduce.2.cloned.1.call-update
  189.9 11.5 %all-gather.9.cloned.1.call-done = f32[128,2048]{1,0:T(8,128)} async-done(((f32[16,2048]{1,0:T(8,128)}), f32[128,2048]{1,0:T(8,128)}) %all-gather.9.cloned.1.call-update) | async-done | bytes 1048592 | tf_op jit(solution)/shard_map/all_gather | solution.py:75
  201.4 1.9 reduce_sum.9
  203.4 65.2 %reduce-scatter.2.cloned.1.call-done = f32[128,3584]{1,0:T(8,128)} async-done(((f32[512,3584]{1,0:T(8,128)}), f32[128,3584]{1,0:T(8,128)}) %reduce-scatter.2.cloned.1.call-update) | async-done | bytes 1835024 | tf_op jit(solution)/shard_map/reduce_scatter | solution.py:23
  268.5 2.5 convert_element_type.44
  271.0 32.5 %all-reduce.2.cloned.1.call-done = f32[3584,16]{0,1:T(8,128)} async-done(((f32[3584,16]{0,1:T(8,128)}), f32[3584,16]{0,1:T(8,128)}) %all-reduce.2.cloned.1.call-update) | async-done | bytes 229392 | tf_op jit(solution)/shard_map/psum | solution.py:77
  303.5 1.6 copy.11
  (1 shorter events, 0.0 us)
Async XLA Ops:
  7.2 143.0 %copy-start = (bf16[3584,16]{0,1:T(8,128)(2,1)S(1)}, bf16[3584,16]{0,1:T(8,128)(2,1)}, u32[]{:S(2)}) copy-start(bf16[3584,16]{0,1:T(8,128)(2,1)} %param.10) | copy-start | bytes 344068
  7.2 102.5 %all-gather.7.cloned.1.call-start = ((), (), s32[]{:S(2)}) async-start(), calls=%async_computation.2 | async-start | bytes 2359296 | tf_op jit(solution)/shard_map/all_gather | solution.py:57
  7.9 101.7 %all-gather.5.cloned.1.call-start = ((), (), s32[]{:S(2)}) async-start(), calls=%async_computation.1 | async-start | bytes 4587520 | tf_op jit(solution)/shard_map/all_gather | solution.py:35
  8.7 192.7 %all-gather.9.cloned.1.call-start = ((), (), s32[]{:S(2)}) async-start(), calls=%async_computation.5 | async-start | bytes 1179648 | tf_op jit(solution)/shard_map/all_gather | solution.py:75
  8.7 14.2 %slice-start = ((s8[7340032]{0:T(1024)(128)(4,1)}), s8[4194304]{0:T(1024)(128)(4,1)S(1)}, s32[]{:S(2)}) async-start(s8[7340032]{0:T(1024)(128)(4,1)} %bitcast.20), calls=%async_computation.6 | async-start | bytes 8388608
  16.4 6.5 %slice-start.1 = ((s8[7340032]{0:T(1024)(128)(4,1)}), s8[3145728]{0:T(1024)(128)(4,1)S(1)}, s32[]{:S(2)}) async-start(s8[7340032]{0:T(1024)(128)(4,1)} %bitcast.20), calls=%async_computation.7 | async-start | bytes 6291456
  150.2 8.1 %copy-start.1 = (bf16[16,2048]{1,0:T(8,128)(2,1)S(1)}, bf16[16,2048]{1,0:T(8,128)(2,1)}, u32[]{:S(2)}) copy-start(bf16[16,2048]{1,0:T(8,128)(2,1)} %param.11) | copy-start | bytes 196612
  150.2 8.1 %copy-start.2 = (bf16[512,2048]{1,0:T(8,128)(2,1)S(1)}, bf16[512,2048]{1,0:T(8,128)(2,1)}, u32[]{:S(2)}) copy-start(bf16[512,2048]{1,0:T(8,128)(2,1)} %all-gather.7.cloned.1.call-done) | copy-start | bytes 6291460
  158.2 110.3 %reduce-scatter.2.cloned.1.call-start = ((), (), s32[]{:S(2)}) async-start(), calls=%async_computation.3 | async-start | bytes 9175040 | tf_op jit(solution)/shard_map/reduce_scatter | solution.py:23
  179.8 123.7 %all-reduce.2.cloned.1.call-start = ((), (), s32[]{:S(2)}) async-start(), calls=%async_computation.4 | async-start | bytes 458752 | tf_op jit(solution)/shard_map/psum | solution.py:77
Sparse Core Ops, SparseCore 0:
  10.1 51.7 all-gather.6
  63.5 29.9 all-gather.4
  158.3 43.0 all-gather.8
  203.8 64.6 reduce-scatter.1
  271.3 32.1 all-reduce.1
